TPU v7x, 32 devices: a whole 2x2x4 slice. The times are simulated.
32 devices in a mesh: row: 16 (over z, y, x), feat: 2 (over core).
Axes of the slice: x: 2, y: 2, z: 4, core: 2. Of those that a mesh axis runs over, the one named last changes fastest.
Arguments:
- codes: int32 [8192, 2048], P('row', 'feat'), may hold values from 0 to 255
- nodes: int32 [8192], P('row'), may hold values from 0 to 3
- labels: int32 [8192], P('row'), may hold values 0 or 1
- weights: float32 [2048], P('feat'), may hold values from -0.125 to 0.125
Outputs:
- gain: float32 [4, 2048, 256], P(None, ('feat', 'row'))
All inputs are finite; a program needn't handle non-finite values. No bound on the sum of `labels` on one device may be relied on, other than what follows from the above.
Results may differ from a plain program's by a relative error of at most 0.0047.
Values sent between devices are 32-bit elements; how exact they have to be, the bound alone decides.
A program may use at most 64 MiB of HBM per device.

v0:
```python
import functools
import math

import jax
import jax.numpy as jnp
from jax import lax
from jax.experimental import pallas as pl
from jax.experimental.pallas import tpu as pltpu
from jax.sharding import PartitionSpec as P

BINS = 256
NODES = 4
STATS = 2 * NODES
HIGH = 4
LOW = BINS // HIGH
TILE = 16
LANES = 128
AHEAD = 3


def kernel(
    halves,
    inner,
    feats,
    turn,
    given_ref,
    weights_ref,
    nodes_ref,
    labels_ref,
    gain_ref,
    raw_ref,
    turned_ref,
    margin_ref,
    code_buf,
    margin_buf,
    stat_buf,
    high_ref,
    low_ref,
    acc_ref,
    left_ref,
    peer_ref,
    raw_sem,
    own_sem,
    code_send,
    code_recv,
    margin_send,
    margin_recv,
    stat_send,
    stat_recv,
    left_send,
    left_recv,
):
    parts, size, rows = turned_ref.shape[1:] if turn else given_ref.shape[1:]
    codes_ref = turned_ref if turn else given_ref
    chunks = halves * parts
    batch = math.gcd(inner, 4)
    me_row = lax.axis_index("row")
    me_feat = lax.axis_index("feat")
    me_out = me_row // inner
    me_in = me_row % inner

    def peer(k):
        return me_out * inner + (me_in + k) % inner

    partner = ((me_out + 1) % halves) * inner + me_in

    def owner(chunk, k):
        half = (me_out + halves - 1 - chunk // parts) % halves
        return half * inner + (me_in + k) % inner

    def code_copy(chunk, k):
        return pltpu.make_async_remote_copy(
            src_ref=codes_ref.at[owner(chunk, k), chunk % parts],
            dst_ref=code_buf.at[chunk, k],
            send_sem=code_send.at[chunk, k],
            recv_sem=code_recv.at[chunk, k],
            device_id={"row": peer(k)},
            device_id_type=pl.DeviceIdType.MESH,
        )

    def own_copy(chunk):
        return pltpu.make_async_copy(
            codes_ref.at[owner(chunk, 0), chunk % parts], code_buf.at[chunk, 0], own_sem.at[chunk]
        )

    def margin_copy(k):
        return pltpu.make_async_remote_copy(
            src_ref=margin_ref,
            dst_ref=margin_buf.at[k],
            send_sem=margin_send.at[k],
            recv_sem=margin_recv.at[k],
            device_id={"feat": (me_feat + k) % feats},
            device_id_type=pl.DeviceIdType.MESH,
        )

    def stat_copy(k):
        return pltpu.make_async_remote_copy(
            src_ref=stat_buf.at[0],
            dst_ref=stat_buf.at[k],
            send_sem=stat_send.at[k],
            recv_sem=stat_recv.at[k],
            device_id={"row": peer(k)},
            device_id_type=pl.DeviceIdType.MESH,
        )

    def left_copy(chunk):
        return pltpu.make_async_remote_copy(
            src_ref=left_ref.at[chunk],
            dst_ref=peer_ref.at[chunk],
            send_sem=left_send.at[chunk],
            recv_sem=left_recv.at[chunk],
            device_id={"row": partner},
            device_id_type=pl.DeviceIdType.MESH,
        )

    def each(low, high, body):
        def step(i, carry):
            body(i)
            return carry

        lax.fori_loop(low, high, step, 0)

    if turn:
        blocks = raw_ref.shape[0]
        per = LANES // (parts * size)
        first_block = ((me_out + halves - 1) % halves) * (blocks // halves)

        def raw_copy(t):
            column = pl.multiple_of((first_block + t) % blocks * LANES, LANES)
            return pltpu.make_async_copy(
                given_ref.at[:, pl.ds(column, LANES)], raw_ref.at[t], raw_sem.at[t]
            )

        for t in range(blocks):
            raw_copy(t).start()
        part = [jnp.zeros((1, rows), jnp.float32)]

        def turn_block(t):
            raw_copy(t).wait()
            turned = jnp.transpose(raw_ref[t].astype(jnp.float32))
            block = (first_block + t) % blocks
            turned_ref[pl.ds(block * per, per)] = turned.reshape(per, parts, size, rows)
            centred = (turned - (BINS - 1) / 2.0).astype(jnp.bfloat16)
            weight = weights_ref[:, pl.ds(pl.multiple_of(block * LANES, LANES), LANES)]
            coarse = weight.astype(jnp.bfloat16).astype(jnp.float32)
            rest = weight - coarse
            middle = rest.astype(jnp.bfloat16).astype(jnp.float32)
            line = lax.broadcasted_iota(jnp.int32, (TILE, LANES), 0)
            split = jnp.where(
                line == 0,
                coarse,
                jnp.where(line == 1, middle, jnp.where(line == 2, rest - middle, 0.0)),
            ).astype(jnp.bfloat16)
            product = jnp.dot(split, centred, preferred_element_type=jnp.float32)
            part[0] = part[0] + (product[0:1] + (product[1:2] + product[2:3])) * (2.0 / BINS)

    barrier = pltpu.get_barrier_semaphore()
    each(
        1,
        inner,
        lambda k: pl.semaphore_signal(
            barrier, inc=1, device_id={"row": peer(k)}, device_id_type=pl.DeviceIdType.MESH
        ),
    )
    each(
        1,
        feats,
        lambda k: pl.semaphore_signal(
            barrier,
            inc=1,
            device_id={"feat": (me_feat + k) % feats},
            device_id_type=pl.DeviceIdType.MESH,
        ),
    )
    if halves > 1:
        pl.semaphore_signal(
            barrier, inc=1, device_id={"row": partner}, device_id_type=pl.DeviceIdType.MESH
        )

    def barrier_wait():
        pl.semaphore_wait(barrier, inner - 1 + feats - 1 + halves - 1)

    def send_chunk(chunk):
        own_copy(chunk).start()
        each(1, inner, lambda k: code_copy(chunk, k).start())

    if turn:
        for t in range(blocks // halves):
            turn_block(t)
        barrier_wait()
        send_chunk(0)
        for t in range(blocks // halves, blocks):
            turn_block(t)
        margin_ref[...] = part[0]
    else:
        margin_ref[...] = weights_ref[...]
        barrier_wait()
        send_chunk(0)
    each(1, feats, lambda k: margin_copy(k).start())
    margin = margin_ref[...]
    for k in range(1, feats):
        margin_copy(k).wait_recv()
        margin = margin + margin_buf[k]
    prob = 1.0 / (1.0 + jnp.exp(-margin))
    grad = prob - labels_ref[...].astype(jnp.float32)
    hess = prob * (1.0 - prob)
    node = lax.broadcasted_iota(jnp.int32, (NODES, rows), 0)
    member = (nodes_ref[...] == node).astype(jnp.float32)
    stat_buf[0] = jnp.concatenate([member * grad, member * hess], 0)
    each(1, inner, lambda k: stat_copy(k).start())
    for chunk in range(1, AHEAD):
        send_chunk(chunk)
    each(1, inner, lambda k: stat_copy(k).wait_recv())

    sub = lax.broadcasted_iota(jnp.int32, (TILE, rows), 0)
    high_id = (sub // STATS).astype(jnp.float32).astype(jnp.bfloat16)
    low_id = sub.astype(jnp.float32).astype(jnp.bfloat16)
    zero = jnp.zeros((TILE, rows), jnp.bfloat16)
    one = jnp.ones((TILE, rows), jnp.bfloat16)

    def chunk_step(chunk):
        @pl.when(chunk + AHEAD < chunks)
        def _():
            send_chunk(chunk + AHEAD)

        acc_ref[...] = jnp.zeros_like(acc_ref)
        own_copy(chunk).wait()

        def batch_step(j):
            first = j * batch
            for q in range(batch):
                if q == 0:
                    @pl.when(j > 0)
                    def _():
                        code_copy(chunk, first).wait_recv()
                else:
                    code_copy(chunk, first + q).wait_recv()
                codes = code_buf[chunk, first + q]
                high = jnp.floor(codes * (1.0 / LOW))
                high_ref[q] = high
                low_ref[q] = codes - high * LOW
            stats = []
            for q in range(batch):
                s = stat_buf[first + q]
                stats.append(jnp.concatenate([s] * (TILE // STATS), 0).astype(jnp.bfloat16))
            for f in range(size):
                aa, bb = [], []
                for q in range(batch):
                    h = jnp.broadcast_to(high_ref[q, f : f + 1, :], (TILE, rows)).astype(jnp.bfloat16)
                    l = jnp.broadcast_to(low_ref[q, f : f + 1, :], (TILE, rows)).astype(jnp.bfloat16)
                    aa.append(
                        jnp.concatenate(
                            [
                                jnp.where(h == high_id + jnp.bfloat16(i * (TILE // STATS)), stats[q], zero)
                                for i in range(HIGH * STATS // TILE)
                            ],
                            0,
                        )
                    )
                    bb.append(
                        jnp.concatenate(
                            [
                                jnp.where(l <= low_id + jnp.bfloat16(i * TILE), one, zero)
                                for i in range(LOW // TILE)
                            ],
                            0,
                        )
                    )
                acc_ref[f] += lax.dot_general(
                    jnp.concatenate(aa, 1),
                    jnp.concatenate(bb, 1),
                    (((1,), (1,)), ((), ())),
                    preferred_element_type=jnp.float32,
                )

        each(0, inner // batch, batch_step)
        for f in range(size):
            acc = acc_ref[f]
            total = jnp.zeros((STATS, 1), jnp.float32)
            pieces = []
            for h in range(HIGH):
                piece = acc[h * STATS : (h + 1) * STATS] + total
                pieces.append(piece)
                total = piece[:, LOW - 1 : LOW]
            left_ref[chunk, f] = jnp.concatenate(pieces, 1)

        if halves > 1:
            @pl.when(chunk < parts)
            def _():
                left_copy(chunk).start()

    each(0, chunks, chunk_step)

    for c in range(parts):
        if halves > 1:
            left_copy(c).wait_recv()
        lam = 1.0
        paired = size % 2 == 0
        for f in range(0, size, 2 if paired else 1):
            grads, hesses = [], []
            for g in range(f, f + 2 if paired else f + 1):
                left = left_ref[chunks - parts + c, g]
                if halves > 1:
                    left = left + peer_ref[c, g]
                grads.append(left[:NODES])
                hesses.append(left[NODES:])
            gl = jnp.concatenate(grads, 0)
            hl = jnp.concatenate(hesses, 0)
            gt, ht = gl[:, BINS - 1 : BINS], hl[:, BINS - 1 : BINS]
            gain = 0.5 * (
                gl * gl / (hl + lam) + (gt - gl) ** 2 / (ht - hl + lam) - gt * gt / (ht + lam)
            )
            for g in range(len(grads)):
                gain_ref[:, c * size + f + g, :] = gain[g * NODES : (g + 1) * NODES]

    each(1, feats, lambda k: margin_copy(k).wait_send())
    each(1, inner, lambda k: stat_copy(k).wait_send())
    each(0, chunks, lambda c: each(1, inner, lambda k: code_copy(c, k).wait_send()))
    if halves > 1:
        each(0, parts, lambda c: left_copy(c).wait_send())


def shards(codes, nodes, labels, weights):
    row_count, feat_count = codes.shape
    groups = lax.axis_size("row")
    feats = lax.axis_size("feat")
    owned = feat_count // groups
    halves = math.gcd(groups, 2)
    inner = groups // halves
    parts = math.gcd(owned, 4)
    size = owned // parts
    turn = size % 8 == 0 and LANES % owned == 0 and feat_count % (LANES * halves) == 0
    if turn:
        given, vector = codes, weights[None, :]
    else:
        value = (codes.astype(jnp.float32) - (BINS - 1) / 2.0) * (2.0 / BINS)
        vector = jnp.dot(value, weights, precision=lax.Precision.HIGHEST)[None, :]
        given = codes.T.reshape(groups, parts, size, row_count).astype(jnp.float32)
    blocks = feat_count // LANES if turn else 1
    chunks = halves * parts
    batch = math.gcd(inner, 4)
    dma = pltpu.SemaphoreType.DMA
    return pl.pallas_call(
        functools.partial(kernel, halves, inner, feats, turn),
        in_specs=[pl.BlockSpec(memory_space=pl.ANY if turn else pltpu.VMEM)]
        + [pl.BlockSpec(memory_space=pltpu.VMEM)] * 3,
        out_specs=pl.BlockSpec(memory_space=pltpu.VMEM),
        out_shape=jax.ShapeDtypeStruct((NODES, owned, BINS), jnp.float32),
        scratch_shapes=[
            pltpu.VMEM((blocks, row_count, LANES) if turn else (1, 8, LANES), jnp.int32),
            pltpu.VMEM((groups, parts, size, row_count) if turn else (1, 1, 8, LANES), jnp.float32),
            pltpu.VMEM((1, row_count), jnp.float32),
            pltpu.VMEM((chunks, inner, size, row_count), jnp.float32),
            pltpu.VMEM((feats, 1, row_count), jnp.float32),
            pltpu.VMEM((inner, STATS, row_count), jnp.float32),
            pltpu.VMEM((batch, size, row_count), jnp.float32),
            pltpu.VMEM((batch, size, row_count), jnp.float32),
            pltpu.VMEM((size, HIGH * STATS, LOW), jnp.float32),
            pltpu.VMEM((chunks, size, STATS, BINS), jnp.float32),
            pltpu.VMEM((parts, size, STATS, BINS), jnp.float32),
            dma((blocks,)),
            dma((chunks,)),
            dma((chunks, inner)),
            dma((chunks, inner)),
            dma((feats,)),
            dma((feats,)),
            dma((inner,)),
            dma((inner,)),
            dma((parts,)),
            dma((parts,)),
        ],
        compiler_params=pltpu.CompilerParams(collective_id=0, has_side_effects=True),
    )(given, vector, nodes[None, :], labels[None, :])


def solution(mesh):
    placed = (P("row", "feat"), P("row"), P("row"), P("feat"))
    return jax.shard_map(
        shards,
        mesh=mesh,
        in_specs=placed,
        out_specs=P(None, ("feat", "row"), None),
        check_vma=False,
    )
```

profile of v0, /device:TPU:0, one launch (start us, length us, event | category | flops | bytes accessed | tf_op | source)
XLA Modules:
  0.0 49.4 jit_solution(465947890818562309)
XLA Ops:
  0.0 47.7 %shard_map.46 = f32[4,64,256]{2,1,0:T(8,128)} custom-call(s32[512,1024]{1,0:T(8,128)} %given_ref.1, f32[1,1024]{1,0:T(1,128)} %bitcast.3, s32[1,512]{1,0:T(1,128)} %bitcast.4, s32[1,512]{1,0:T(1,128)} %bitcast.5), custom_call_target="tpu_custom_call" | custom-call | tf_op jit(solution)/shard_map/pallas_call | solution.py:343
  47.7 1.7 %copy.6 = f32[4,64,256]{2,1,0:T(8,128)} copy(f32[4,64,256]{2,1,0:T(8,128)} %shard_map.46) | data formatting | bytes 524288
where the time goes:
time: 49.6 us; the launch traced here: 49.4 us
  Pallas kernels  47.7 us (96%)
  local copies, waits for them, and re-layouts  1.67 us (3%)
    pallas_call x1, Pallas kernels, shards(): pl.pallas_call(functools.partial(kernel, halves, inner, feats, turn), in_...  47.7 us
    unnamed x1, local copies, waits for them, and re-layouts  1.67 us

commit v1 on v0

--- a/solution.py
+++ b/solution.py
@@ -373,12 +373,538 @@
     )(given, vector, nodes[None, :], labels[None, :])
 
 
+PLANES = 4
+CHUNK = 8
+EARLY = 2
+AHEAD_PLANE = 6
+DELAY_INNER_AWAY = 4
+DELAY_INNER_HOME = 9
+DELAY_OUTER_HOME = 13
+
+
+def plane_kernel(
+    n,
+    feats,
+    early,
+    given_ref,
+    weights_ref,
+    nodes_ref,
+    labels_ref,
+    gain_ref,
+    raw_ref,
+    turned_ref,
+    margin_ref,
+    code_buf,
+    margin_buf,
+    stat_buf,
+    high_ref,
+    low_ref,
+    hist_buf,
+    come_buf,
+    gain_own,
+    gain_out,
+    gain_in,
+    raw_sem,
+    own_sem,
+    code_send,
+    code_recv,
+    margin_send,
+    margin_recv,
+    stat_send,
+    stat_recv,
+    hist_send,
+    hist_recv,
+    gain_send,
+    gain_recv,
+    out_sem,
+):
+    parts, size, rows = turned_ref.shape[1:]
+    blocks = raw_ref.shape[0]
+    per = LANES // (parts * size)
+    block_span = n // per
+    steps = 4 * parts
+    me_row = lax.axis_index("row")
+    me_feat = lax.axis_index("feat")
+    plane = me_row // n
+    me_in = me_row % n
+    half = plane // 2
+    inner_plane = 1 + half
+    outer_plane = 3 * half
+    outer = plane == outer_plane
+    inner = plane == inner_plane
+
+    def each(low, high, body):
+        def step(i, carry):
+            body(i)
+            return carry
+
+        lax.fori_loop(low, high, step, 0)
+
+    def spot(k):
+        return (me_in + k) % n
+
+    def away(i):
+        return i % 2 == 0
+
+    def is_early(i):
+        return jnp.logical_and(away(i), i // 2 < early)
+
+    def group_of(i):
+        base = jnp.where(i // 2 < parts, inner_plane, outer_plane)
+        return jnp.where(away(i), PLANES - 1 - base, base)
+
+    def part_of(i):
+        return (i // 2) % parts
+
+    def remote(src, dst, send, recv, row):
+        return pltpu.make_async_remote_copy(
+            src_ref=src,
+            dst_ref=dst,
+            send_sem=send,
+            recv_sem=recv,
+            device_id={"row": row},
+            device_id_type=pl.DeviceIdType.MESH,
+        )
+
+    def code_copy(i, k):
+        return remote(
+            turned_ref.at[group_of(i) * n + spot(k), part_of(i)],
+            code_buf.at[i, k],
+            code_send.at[i, k],
+            code_recv.at[i, k],
+            plane * n + spot(k),
+        )
+
+    def early_copy(i, k):
+        slot = steps + i // 2
+        return remote(
+            turned_ref.at[group_of(i) * n + spot(k), part_of(i)],
+            code_buf.at[slot, k],
+            code_send.at[slot, k],
+            code_recv.at[slot, k],
+            inner_plane * n + spot(k),
+        )
+
+    def own_copy(i):
+        return pltpu.make_async_copy(
+            turned_ref.at[group_of(i) * n + me_in, part_of(i)], code_buf.at[i, 0], own_sem.at[i]
+        )
+
+    def margin_copy(k):
+        return pltpu.make_async_remote_copy(
+            src_ref=margin_ref,
+            dst_ref=margin_buf.at[k],
+            send_sem=margin_send.at[k],
+            recv_sem=margin_recv.at[k],
+            device_id={"feat": (me_feat + k) % feats},
+            device_id_type=pl.DeviceIdType.MESH,
+        )
+
+    def stat_copy(k):
+        return remote(
+            stat_buf.at[0], stat_buf.at[k], stat_send.at[k], stat_recv.at[k], plane * n + spot(k)
+        )
+
+    def stat_in_copy(k):
+        return remote(
+            stat_buf.at[0],
+            stat_buf.at[n + k],
+            stat_send.at[n + k],
+            stat_recv.at[n + k],
+            inner_plane * n + spot(k),
+        )
+
+    def hist_copy(i):
+        far = jnp.where(outer, inner_plane, jnp.where(away(i), PLANES - 1 - plane, outer_plane))
+        there = jnp.where(jnp.logical_and(inner, away(i)), i + 1, i)
+        return remote(
+            hist_buf.at[i], come_buf.at[there], hist_send.at[i], hist_recv.at[there], far * n + me_in
+        )
+
+    def gain_copy(c):
+        return remote(
+            gain_out.at[c], gain_in.at[c], gain_send.at[c], gain_recv.at[c], inner_plane * n + me_in
+        )
+
+    def out_copy(src, c):
+        row = pl.multiple_of(c * size, size)
+        return pltpu.make_async_copy(
+            src.at[c], gain_ref.at[:, pl.ds(row, size), :], out_sem.at[c]
+        )
+
+    order = [
+        PLANES - 1 - inner_plane,
+        inner_plane,
+        PLANES - 1 - outer_plane,
+        outer_plane,
+    ]
+
+    def block_of(t):
+        return order[t // block_span] * block_span + t % block_span
+
+    def raw_copy(t):
+        column = pl.multiple_of(block_of(t) * LANES, LANES)
+        return pltpu.make_async_copy(
+            given_ref.at[:, pl.ds(column, LANES)], raw_ref.at[t], raw_sem.at[t]
+        )
+
+    for t in range(blocks):
+        raw_copy(t).start()
+
+    barrier = pltpu.get_barrier_semaphore()
+
+    def greet(row):
+        pl.semaphore_signal(
+            barrier, inc=1, device_id={"row": row}, device_id_type=pl.DeviceIdType.MESH
+        )
+
+    each(1, n, lambda k: greet(plane * n + spot(k)))
+    facing = jnp.where(outer, inner_plane, outer_plane)
+    each(0, n, lambda k: greet(facing * n + spot(k)))
+
+    @pl.when(inner)
+    def _():
+        greet((PLANES - 1 - plane) * n + me_in)
+
+    each(
+        1,
+        feats,
+        lambda k: pl.semaphore_signal(
+            barrier,
+            inc=1,
+            device_id={"feat": (me_feat + k) % feats},
+            device_id_type=pl.DeviceIdType.MESH,
+        ),
+    )
+
+    def send_chunk(i):
+        relayed = jnp.logical_and(outer, is_early(i))
+
+        @pl.when(relayed)
+        def _():
+            each(0, n, lambda k: early_copy(i, k).start())
+
+        @pl.when(jnp.logical_not(relayed))
+        def _():
+            own_copy(i).start()
+            each(1, n, lambda k: code_copy(i, k).start())
+
+    part_sum = [jnp.zeros((1, rows), jnp.float32)]
+
+    def turn_block(t):
+        raw_copy(t).wait()
+        turned = jnp.transpose(raw_ref[t].astype(jnp.float32))
+        block = block_of(t)
+        turned_ref[pl.ds(block * per, per)] = turned.reshape(per, parts, size, rows)
+        centred = (turned - (BINS - 1) / 2.0).astype(jnp.bfloat16)
+        weight = weights_ref[:, pl.ds(pl.multiple_of(block * LANES, LANES), LANES)]
+        coarse = weight.astype(jnp.bfloat16).astype(jnp.float32)
+        rest = weight - coarse
+        middle = rest.astype(jnp.bfloat16).astype(jnp.float32)
+        line = lax.broadcasted_iota(jnp.int32, (TILE, LANES), 0)
+        split = jnp.where(
+            line == 0,
+            coarse,
+            jnp.where(line == 1, middle, jnp.where(line == 2, rest - middle, 0.0)),
+        ).astype(jnp.bfloat16)
+        product = jnp.dot(split, centred, preferred_element_type=jnp.float32)
+        part_sum[0] = part_sum[0] + (
+            product[0:1] + (product[1:2] + product[2:3])
+        ) * (2.0 / BINS)
+
+    for t in range(block_span):
+        turn_block(t)
+    pl.semaphore_wait(barrier, jnp.where(outer, 2 * n - 1, 2 * n) + feats - 1)
+    each(0, early, lambda a: send_chunk(2 * a))
+    for t in range(block_span, blocks):
+        turn_block(t)
+    margin_ref[...] = part_sum[0]
+    each(1, feats, lambda k: margin_copy(k).start())
+    each(0, early, lambda a: send_chunk(2 * a + 1))
+    margin = margin_ref[...]
+    for k in range(1, feats):
+        margin_copy(k).wait_recv()
+        margin = margin + margin_buf[k]
+    prob = 1.0 / (1.0 + jnp.exp(-margin))
+    grad = prob - labels_ref[...].astype(jnp.float32)
+    hess = prob * (1.0 - prob)
+    node = lax.broadcasted_iota(jnp.int32, (NODES, rows), 0)
+    member = (nodes_ref[...] == node).astype(jnp.float32)
+    stat_buf[0] = jnp.concatenate([member * grad, member * hess], 0)
+    each(1, n, lambda k: stat_copy(k).start())
+
+    @pl.when(outer)
+    def _():
+        each(0, n, lambda k: stat_in_copy(k).start())
+
+    each(2 * early, AHEAD_PLANE, send_chunk)
+    each(1, n, lambda k: stat_copy(k).wait_recv())
+
+    @pl.when(inner)
+    def _():
+        each(0, n, lambda k: stat_in_copy(k).wait_recv())
+
+    sub = lax.broadcasted_iota(jnp.int32, (TILE, rows), 0)
+    high_id = (sub // STATS).astype(jnp.float32).astype(jnp.bfloat16)
+    low_id = sub.astype(jnp.float32).astype(jnp.bfloat16)
+    zero = jnp.zeros((TILE, rows), jnp.bfloat16)
+    one = jnp.ones((TILE, rows), jnp.bfloat16)
+    front = lax.broadcasted_iota(jnp.int32, (STATS, LANES), 1) < LOW
+    front_all = lax.broadcasted_iota(jnp.int32, (HIGH * STATS, LANES), 1) < LOW
+
+    def compute(i):
+        hist_buf[i] = jnp.zeros(hist_buf.shape[1:], jnp.float32)
+
+        def batch_step(b):
+            slot = jnp.where(b == 0, i, steps + i // 2)
+            for q in range(n):
+                if q == 0:
+                    @pl.when(b == 0)
+                    def _():
+                        own_copy(i).wait()
+
+                    @pl.when(b > 0)
+                    def _():
+                        early_copy(i, 0).wait_recv()
+                else:
+                    remote(
+                        turned_ref.at[0, 0],
+                        code_buf.at[slot, q],
+                        code_send.at[slot, q],
+                        code_recv.at[slot, q],
+                        plane * n + spot(q),
+                    ).wait_recv()
+                codes = code_buf[slot, q]
+                high = jnp.floor(codes * (1.0 / LOW))
+                high_ref[q] = high
+                low_ref[q] = codes - high * LOW
+            stats = []
+            for q in range(n):
+                s = stat_buf[b * n + q]
+                stats.append(jnp.concatenate([s] * (TILE // STATS), 0).astype(jnp.bfloat16))
+            for p in range(size // 2):
+                aa, bb = [], []
+                for q in range(n):
+                    a_rows, b_rows = [], []
+                    for f in (2 * p, 2 * p + 1):
+                        h = jnp.broadcast_to(high_ref[q, f : f + 1, :], (TILE, rows)).astype(jnp.bfloat16)
+                        l = jnp.broadcast_to(low_ref[q, f : f + 1, :], (TILE, rows)).astype(jnp.bfloat16)
+                        for t in range(HIGH * STATS // TILE):
+                            a_rows.append(
+                                jnp.where(h == high_id + jnp.bfloat16(t * (TILE // STATS)), stats[q], zero)
+                            )
+                        for t in range(LOW // TILE):
+                            b_rows.append(jnp.where(l <= low_id + jnp.bfloat16(t * TILE), one, zero))
+                    aa.append(jnp.concatenate(a_rows, 0))
+                    bb.append(jnp.concatenate(b_rows, 0))
+                both = lax.dot_general(
+                    jnp.concatenate(aa, 1),
+                    jnp.concatenate(bb, 1),
+                    (((1,), (1,)), ((), ())),
+                    preferred_element_type=jnp.float32,
+                )
+                hist_buf[i, p] += jnp.where(
+                    front_all, both[: HIGH * STATS], both[HIGH * STATS :]
+                )
+
+        each(0, jnp.where(jnp.logical_and(inner, is_early(i)), 2, 1), batch_step)
+
+    def finalise(i, target):
+        lam = 1.0
+        c = part_of(i)
+        for p in range(size // 2):
+            total = jnp.zeros((STATS, LANES), jnp.float32)
+            lines = []
+            for h in range(HIGH):
+                piece = (
+                    hist_buf[i, p, h * STATS : (h + 1) * STATS]
+                    + come_buf[i, p, h * STATS : (h + 1) * STATS]
+                )
+                lines.append(piece + total)
+                if h + 1 < HIGH:
+                    total = total + jnp.where(
+                        front, piece[:, LOW - 1 : LOW], piece[:, 2 * LOW - 1 : 2 * LOW]
+                    )
+            rolled = [pltpu.roll(line, LOW, 1) for line in lines]
+            lefts = [
+                jnp.concatenate(
+                    [jnp.where(front, lines[0], rolled[1]), jnp.where(front, lines[2], rolled[3])], 1
+                ),
+                jnp.concatenate(
+                    [jnp.where(front, rolled[0], lines[1]), jnp.where(front, rolled[2], lines[3])], 1
+                ),
+            ]
+            gl = jnp.concatenate([left[:NODES] for left in lefts], 0)
+            hl = jnp.concatenate([left[NODES:] for left in lefts], 0)
+            gt, ht = gl[:, BINS - 1 : BINS], hl[:, BINS - 1 : BINS]
+            gain = 0.5 * (
+                gl * gl / (hl + lam) + (gt - gl) ** 2 / (ht - hl + lam) - gt * gt / (ht + lam)
+            )
+            for g in range(2):
+                target[c, :, 2 * p + g, :] = gain[g * NODES : (g + 1) * NODES]
+
+    def settle(i):
+        hist_copy_in = remote(
+            hist_buf.at[i], come_buf.at[i], hist_send.at[i], hist_recv.at[i], plane * n + spot(1)
+        )
+        hist_copy_in.wait_recv()
+
+        @pl.when(inner)
+        def _():
+            hist_buf[i] += come_buf[i]
+            hist_copy(i).start()
+
+    delay_home = jnp.where(outer, DELAY_OUTER_HOME, DELAY_INNER_HOME)
+
+    def step(t):
+        @pl.when(t < steps)
+        def _():
+            @pl.when(t + AHEAD_PLANE < steps)
+            def _():
+                send_chunk(t + AHEAD_PLANE)
+
+            @pl.when(jnp.logical_not(jnp.logical_and(outer, is_early(t))))
+            def _():
+                compute(t)
+
+            @pl.when(jnp.logical_and(away(t), is_early(t) == inner))
+            def _():
+                hist_copy(t).start()
+
+        i = t - DELAY_INNER_AWAY
+
+        @pl.when(
+            jnp.logical_and(
+                jnp.logical_and(inner, jnp.logical_and(i >= 2 * early, i < steps)), i % 2 == 0
+            )
+        )
+        def _():
+            settle(i)
+
+        j = t - delay_home
+
+        @pl.when(jnp.logical_and(jnp.logical_and(j >= 0, j < steps), j % 2 == 1))
+        def _():
+            settle(j)
+
+            @pl.when(jnp.logical_and(outer, j // 2 < parts))
+            def _():
+                finalise(j, gain_out)
+                gain_copy(part_of(j)).start()
+
+            @pl.when(jnp.logical_and(outer, j // 2 >= parts))
+            def _():
+                finalise(j, gain_own)
+                out_copy(gain_own, part_of(j)).start()
+
+    each(0, steps + max(DELAY_INNER_AWAY, DELAY_INNER_HOME, DELAY_OUTER_HOME), step)
+
+    @pl.when(inner)
+    def _():
+        def take(c):
+            gain_copy(c).wait_recv()
+            out_copy(gain_in, c).start()
+
+        each(0, parts, take)
+
+    each(1, feats, lambda k: margin_copy(k).wait_send())
+    each(1, n, lambda k: stat_copy(k).wait_send())
+
+    @pl.when(outer)
+    def _():
+        each(0, n, lambda k: stat_in_copy(k).wait_send())
+        each(0, parts, lambda c: gain_copy(c).wait_send())
+        each(0, early, lambda a: each(0, n, lambda k: early_copy(2 * a, k).wait_send()))
+
+    def finish(i):
+        @pl.when(jnp.logical_not(jnp.logical_and(outer, is_early(i))))
+        def _():
+            each(1, n, lambda k: code_copy(i, k).wait_send())
+
+        @pl.when(jnp.logical_or(inner, jnp.logical_and(away(i), jnp.logical_not(is_early(i)))))
+        def _():
+            hist_copy(i).wait_send()
+
+    each(0, steps, finish)
+
+    each(0, parts, lambda c: out_copy(gain_own, c).wait())
+
+
+def plane_shards(codes, nodes, labels, weights):
+    row_count, feat_count = codes.shape
+    groups = lax.axis_size("row")
+    feats = lax.axis_size("feat")
+    owned = feat_count // groups
+    n = groups // PLANES
+    size = CHUNK
+    parts = owned // size
+    blocks = feat_count // LANES
+    steps = 4 * parts
+    early = min(EARLY, parts)
+    dma = pltpu.SemaphoreType.DMA
+    return pl.pallas_call(
+        functools.partial(plane_kernel, n, feats, early),
+        in_specs=[pl.BlockSpec(memory_space=pl.ANY)]
+        + [pl.BlockSpec(memory_space=pltpu.VMEM)] * 3,
+        out_specs=pl.BlockSpec(memory_space=pl.ANY),
+        out_shape=jax.ShapeDtypeStruct((NODES, owned, BINS), jnp.float32),
+        scratch_shapes=[
+            pltpu.VMEM((blocks, row_count, LANES), jnp.int32),
+            pltpu.VMEM((groups, parts, size, row_count), jnp.float32),
+            pltpu.VMEM((1, row_count), jnp.float32),
+            pltpu.VMEM((steps + early, n, size, row_count), jnp.float32),
+            pltpu.VMEM((feats, 1, row_count), jnp.float32),
+            pltpu.VMEM((2 * n, STATS, row_count), jnp.float32),
+            pltpu.VMEM((n, size, row_count), jnp.float32),
+            pltpu.VMEM((n, size, row_count), jnp.float32),
+            pltpu.VMEM((steps, size // 2, HIGH * STATS, LANES), jnp.float32),
+            pltpu.VMEM((steps, size // 2, HIGH * STATS, LANES), jnp.float32),
+            pltpu.VMEM((parts, NODES, size, BINS), jnp.float32),
+            pltpu.VMEM((parts, NODES, size, BINS), jnp.float32),
+            pltpu.VMEM((parts, NODES, size, BINS), jnp.float32),
+            dma((blocks,)),
+            dma((steps,)),
+            dma((steps + early, n)),
+            dma((steps + early, n)),
+            dma((feats,)),
+            dma((feats,)),
+            dma((2 * n,)),
+            dma((2 * n,)),
+            dma((steps,)),
+            dma((steps,)),
+            dma((parts,)),
+            dma((parts,)),
+            dma((parts,)),
+        ],
+        compiler_params=pltpu.CompilerParams(collective_id=0, has_side_effects=True),
+    )(codes, weights[None, :], nodes[None, :], labels[None, :])
+
+
+def fits(mesh, codes):
+    groups, feats = mesh.shape["row"], mesh.shape["feat"]
+    rows, width = codes.shape[0] // groups, codes.shape[1] // feats
+    n, owned = groups // PLANES, width // groups
+    return (
+        groups % PLANES == 0
+        and 1 < n <= PLANES
+        and rows % LANES == 0
+        and owned % CHUNK == 0
+        and LANES % owned == 0
+        and (n * owned) % LANES == 0
+    )
+
+
 def solution(mesh):
     placed = (P("row", "feat"), P("row"), P("row"), P("feat"))
-    return jax.shard_map(
-        shards,
-        mesh=mesh,
-        in_specs=placed,
-        out_specs=P(None, ("feat", "row"), None),
-        check_vma=False,
-    )
+
+    def run(codes, nodes, labels, weights):
+        body = plane_shards if fits(mesh, codes) else shards
+        return jax.shard_map(
+            body,
+            mesh=mesh,
+            in_specs=placed,
+            out_specs=P(None, ("feat", "row"), None),
+            check_vma=False,
+        )(codes, nodes, labels, weights)
+
+    return run

time: 49.6 us -> 65.3 us (1.32)
  Pallas kernels: 47.7 us -> 63.4 us
    pallas_call x1, Pallas kernels: 47.7 us -> 63.4 us  [plane_shards(): pl.pallas_call(functools.partial(plane_kernel, n, feats, early), in_specs...]
where the time goes in v1:
time: 65.3 us; the launch traced here: 65.1 us
  Pallas kernels  63.4 us (97%)
  local copies, waits for them, and re-layouts  1.67 us (3%)
    pallas_call x1, Pallas kernels, plane_shards(): pl.pallas_call(functools.partial(plane_kernel, n, feats, early), in_specs...  63.4 us
    unnamed x1, local copies, waits for them, and re-layouts  1.67 us

profile of v1, /device:TPU:0, one launch (start us, length us, event | category | flops | bytes accessed | tf_op | source)
XLA Modules:
  0.0 65.1 jit_solution(3913488702807269308)
XLA Ops:
  0.0 63.4 %shard_map.46 = f32[4,64,256]{2,1,0:T(8,128)} custom-call(s32[512,1024]{1,0:T(8,128)} %given_ref.1, f32[1,1024]{1,0:T(1,128)} %bitcast.3, s32[1,512]{1,0:T(1,128)} %bitcast.4, s32[1,512]{1,0:T(1,128)} %bitcast.5), custom_call_target="tpu_custom_call" | custom-call | tf_op jit(solution)/shard_map/pallas_call | solution.py:845
  63.4 1.7 %copy.6 = f32[4,64,256]{2,1,0:T(8,128)} copy(f32[4,64,256]{2,1,0:T(8,128)} %shard_map.46) | data formatting | bytes 524288

commit v2 on v0

--- a/solution.py
+++ b/solution.py
@@ -24,16 +24,20 @@
     feats,
     turn,
     given_ref,
+    weights_in,
+    nodes_in,
+    labels_in,
+    gain_ref,
     weights_ref,
     nodes_ref,
     labels_ref,
-    gain_ref,
     raw_ref,
     turned_ref,
     margin_ref,
     code_buf,
     margin_buf,
     stat_buf,
+    wide_ref,
     high_ref,
     low_ref,
     acc_ref,
@@ -49,6 +53,7 @@
     stat_recv,
     left_send,
     left_recv,
+    take_sem,
 ):
     parts, size, rows = turned_ref.shape[1:] if turn else given_ref.shape[1:]
     codes_ref = turned_ref if turn else given_ref
@@ -59,14 +64,27 @@
     me_out = me_row // inner
     me_in = me_row % inner
 
+    def spot(k):
+        if inner & (inner - 1):
+            return (me_in + k) % inner
+        place, bit = 0, 1
+        while bit < inner:
+            place = place + (me_in // bit + k // bit) % 2 * bit
+            bit *= 2
+        return place
+
     def peer(k):
-        return me_out * inner + (me_in + k) % inner
-
-    partner = ((me_out + 1) % halves) * inner + me_in
+        return me_out * inner + spot(k)
+
+    def across(m):
+        return (m + inner // 2) % inner
+
+    partner = ((me_out + 1) % halves) * inner + across(me_in)
 
     def owner(chunk, k):
         half = (me_out + halves - 1 - chunk // parts) % halves
-        return half * inner + (me_in + k) % inner
+        place = spot(k)
+        return half * inner + jnp.where(chunk < chunks - parts, across(place), place)
 
     def code_copy(chunk, k):
         return pltpu.make_async_remote_copy(
@@ -120,25 +138,40 @@
 
         lax.fori_loop(low, high, step, 0)
 
+    takes = [
+        pltpu.make_async_copy(source, target, take_sem.at[i])
+        for i, (source, target) in enumerate(
+            ((weights_in, weights_ref), (nodes_in, nodes_ref), (labels_in, labels_ref))
+        )
+    ]
     if turn:
         blocks = raw_ref.shape[0]
+        near = blocks // halves
         per = LANES // (parts * size)
         first_block = ((me_out + halves - 1) % halves) * (blocks // halves)
 
+        def block_of(t):
+            if t < near:
+                return (first_block + (t + me_in * 2 // inner * (near // 2)) % near) % blocks
+            return (first_block + t) % blocks
+
         def raw_copy(t):
-            column = pl.multiple_of((first_block + t) % blocks * LANES, LANES)
+            column = pl.multiple_of(block_of(t) * LANES, LANES)
             return pltpu.make_async_copy(
                 given_ref.at[:, pl.ds(column, LANES)], raw_ref.at[t], raw_sem.at[t]
             )
 
-        for t in range(blocks):
+        raw_copy(0).start()
+        for take in takes:
+            take.start()
+        for t in range(1, blocks):
             raw_copy(t).start()
         part = [jnp.zeros((1, rows), jnp.float32)]
 
         def turn_block(t):
             raw_copy(t).wait()
             turned = jnp.transpose(raw_ref[t].astype(jnp.float32))
-            block = (first_block + t) % blocks
+            block = block_of(t)
             turned_ref[pl.ds(block * per, per)] = turned.reshape(per, parts, size, rows)
             centred = (turned - (BINS - 1) / 2.0).astype(jnp.bfloat16)
             weight = weights_ref[:, pl.ds(pl.multiple_of(block * LANES, LANES), LANES)]
@@ -154,6 +187,9 @@
             product = jnp.dot(split, centred, preferred_element_type=jnp.float32)
             part[0] = part[0] + (product[0:1] + (product[1:2] + product[2:3])) * (2.0 / BINS)
 
+    else:
+        for take in takes:
+            take.start()
     barrier = pltpu.get_barrier_semaphore()
     each(
         1,
@@ -182,17 +218,31 @@
 
     def send_chunk(chunk):
         own_copy(chunk).start()
-        each(1, inner, lambda k: code_copy(chunk, k).start())
+        each(1, inner, lambda k: code_copy(chunk, inner - k).start())
 
     if turn:
-        for t in range(blocks // halves):
+        takes[0].wait()
+        for t in range(near):
             turn_block(t)
-        barrier_wait()
-        send_chunk(0)
-        for t in range(blocks // halves, blocks):
+            if t == 0:
+                barrier_wait()
+            for o in range(per):
+                place = (block_of(t) * per + o) % inner
+                k = spot(across(place) if halves > 1 else place)
+
+                @pl.when(k == 0)
+                def _():
+                    own_copy(0).start()
+
+                @pl.when(k > 0)
+                def _():
+                    code_copy(0, k).start()
+
+        for t in range(near, blocks):
             turn_block(t)
         margin_ref[...] = part[0]
     else:
+        takes[0].wait()
         margin_ref[...] = weights_ref[...]
         barrier_wait()
         send_chunk(0)
@@ -201,18 +251,21 @@
     for k in range(1, feats):
         margin_copy(k).wait_recv()
         margin = margin + margin_buf[k]
+    takes[1].wait()
+    takes[2].wait()
     prob = 1.0 / (1.0 + jnp.exp(-margin))
     grad = prob - labels_ref[...].astype(jnp.float32)
     hess = prob * (1.0 - prob)
-    node = lax.broadcasted_iota(jnp.int32, (NODES, rows), 0)
-    member = (nodes_ref[...] == node).astype(jnp.float32)
-    stat_buf[0] = jnp.concatenate([member * grad, member * hess], 0)
+    stat_buf[0, 0] = grad
+    stat_buf[0, 1] = hess
+    stat_buf[0, 2] = nodes_ref[...].astype(jnp.float32)
     each(1, inner, lambda k: stat_copy(k).start())
     for chunk in range(1, AHEAD):
         send_chunk(chunk)
-    each(1, inner, lambda k: stat_copy(k).wait_recv())
 
     sub = lax.broadcasted_iota(jnp.int32, (TILE, rows), 0)
+    node_id = (sub % NODES).astype(jnp.float32)
+    is_grad = sub % STATS < NODES
     high_id = (sub // STATS).astype(jnp.float32).astype(jnp.bfloat16)
     low_id = sub.astype(jnp.float32).astype(jnp.bfloat16)
     zero = jnp.zeros((TILE, rows), jnp.bfloat16)
@@ -239,10 +292,23 @@
                 high = jnp.floor(codes * (1.0 / LOW))
                 high_ref[q] = high
                 low_ref[q] = codes - high * LOW
-            stats = []
-            for q in range(batch):
-                s = stat_buf[first + q]
-                stats.append(jnp.concatenate([s] * (TILE // STATS), 0).astype(jnp.bfloat16))
+            @pl.when(chunk == 0)
+            def _():
+                for q in range(batch):
+                    if q == 0:
+                        @pl.when(j > 0)
+                        def _():
+                            stat_copy(first).wait_recv()
+                    else:
+                        stat_copy(first + q).wait_recv()
+                    member = stat_buf[first + q, 2] == node_id
+                    wide_ref[first + q] = jnp.where(
+                        member,
+                        jnp.where(is_grad, stat_buf[first + q, 0], stat_buf[first + q, 1]),
+                        0.0,
+                    ).astype(jnp.bfloat16)
+
+            stats = [wide_ref[first + q] for q in range(batch)]
             for f in range(size):
                 aa, bb = [], []
                 for q in range(batch):
@@ -329,7 +395,12 @@
     inner = groups // halves
     parts = math.gcd(owned, 4)
     size = owned // parts
-    turn = size % 8 == 0 and LANES % owned == 0 and feat_count % (LANES * halves) == 0
+    turn = (
+        size % 8 == 0
+        and LANES % owned == 0
+        and feat_count % (LANES * halves) == 0
+        and inner & (inner - 1) == 0
+    )
     if turn:
         given, vector = codes, weights[None, :]
     else:
@@ -343,16 +414,20 @@
     return pl.pallas_call(
         functools.partial(kernel, halves, inner, feats, turn),
         in_specs=[pl.BlockSpec(memory_space=pl.ANY if turn else pltpu.VMEM)]
-        + [pl.BlockSpec(memory_space=pltpu.VMEM)] * 3,
+        + [pl.BlockSpec(memory_space=pl.ANY)] * 3,
         out_specs=pl.BlockSpec(memory_space=pltpu.VMEM),
-        out_shape=jax.ShapeDtypeStruct((NODES, owned, BINS), jnp.float32),
+        out_shape=pltpu.VMEM((NODES, owned, BINS), jnp.float32),
         scratch_shapes=[
+            pltpu.VMEM(vector.shape, jnp.float32),
+            pltpu.VMEM((1, row_count), jnp.int32),
+            pltpu.VMEM((1, row_count), jnp.int32),
             pltpu.VMEM((blocks, row_count, LANES) if turn else (1, 8, LANES), jnp.int32),
             pltpu.VMEM((groups, parts, size, row_count) if turn else (1, 1, 8, LANES), jnp.float32),
             pltpu.VMEM((1, row_count), jnp.float32),
             pltpu.VMEM((chunks, inner, size, row_count), jnp.float32),
             pltpu.VMEM((feats, 1, row_count), jnp.float32),
-            pltpu.VMEM((inner, STATS, row_count), jnp.float32),
+            pltpu.VMEM((inner, 3, 1, row_count), jnp.float32),
+            pltpu.VMEM((inner, TILE, row_count), jnp.bfloat16),
             pltpu.VMEM((batch, size, row_count), jnp.float32),
             pltpu.VMEM((batch, size, row_count), jnp.float32),
             pltpu.VMEM((size, HIGH * STATS, LOW), jnp.float32),
@@ -368,6 +443,7 @@
             dma((inner,)),
             dma((parts,)),
             dma((parts,)),
+            dma((3,)),
         ],
         compiler_params=pltpu.CompilerParams(collective_id=0, has_side_effects=True),
     )(given, vector, nodes[None, :], labels[None, :])

time: 49.6 us -> 45.5 us (0.917)
  Pallas kernels: 47.7 us -> 44.6 us
  local copies, waits for them, and re-layouts: 1.67 us -> 0.71 us
    pallas_call x1, Pallas kernels: 47.7 us -> 44.6 us  [shards(): pl.pallas_call(functools.partial(kernel, halves, inner, feats, turn), in_...]
    unnamed x1, local copies, waits for them, and re-layouts: 1.67 us -> 0.71 us
where the time goes in v2:
time: 45.5 us; the launch traced here: 45.3 us
  Pallas kernels  44.6 us (98%)
  local copies, waits for them, and re-layouts  0.71 us (2%)
    pallas_call x1, Pallas kernels, shards(): pl.pallas_call(functools.partial(kernel, halves, inner, feats, turn), in_...  44.6 us

profile of v2, /device:TPU:0, one launch (start us, length us, event | category | flops | bytes accessed | tf_op | source)
XLA Modules:
  0.0 45.3 jit_solution(15668454678831165144)
XLA Ops:
  0.0 44.6 %shard_map.46 = f32[4,64,256]{2,1,0:T(8,128)S(1)} custom-call(s32[512,1024]{1,0:T(8,128)} %given_ref.1, f32[1,1024]{1,0:T(1,128)} %bitcast.3, s32[1,512]{1,0:T(1,128)} %bitcast.4, s32[1,512]{1,0:T(1,128)} %bitcast.5), custom_call_target="tpu_custom_call" | custom-call | tf_op jit(solution)/shard_map/pallas_call | solution.py:414
  44.6 0.7 %copy.6 = f32[4,64,256]{2,1,0:T(8,128)} copy(f32[4,64,256]{2,1,0:T(8,128)S(1)} %shard_map.46) | data formatting | bytes 524288

commit v3 on v2

--- a/solution.py
+++ b/solution.py
@@ -161,11 +161,6 @@
                 given_ref.at[:, pl.ds(column, LANES)], raw_ref.at[t], raw_sem.at[t]
             )
 
-        raw_copy(0).start()
-        for take in takes:
-            take.start()
-        for t in range(1, blocks):
-            raw_copy(t).start()
         part = [jnp.zeros((1, rows), jnp.float32)]
 
         def turn_block(t):
@@ -187,9 +182,6 @@
             product = jnp.dot(split, centred, preferred_element_type=jnp.float32)
             part[0] = part[0] + (product[0:1] + (product[1:2] + product[2:3])) * (2.0 / BINS)
 
-    else:
-        for take in takes:
-            take.start()
     barrier = pltpu.get_barrier_semaphore()
     each(
         1,
@@ -212,6 +204,16 @@
         pl.semaphore_signal(
             barrier, inc=1, device_id={"row": partner}, device_id_type=pl.DeviceIdType.MESH
         )
+
+    if turn:
+        raw_copy(0).start()
+        for take in takes:
+            take.start()
+        for t in range(1, blocks):
+            raw_copy(t).start()
+    else:
+        for take in takes:
+            take.start()
 
     def barrier_wait():
         pl.semaphore_wait(barrier, inner - 1 + feats - 1 + halves - 1)

time: 45.5 us -> 45.3 us (level)
  no operation moved by 1% of the time
where the time goes in v3:
time: 45.3 us; the launch traced here: 45.2 us
  Pallas kernels  44.5 us (98%)
  local copies, waits for them, and re-layouts  0.71 us (2%)
    pallas_call x1, Pallas kernels, shards(): pl.pallas_call(functools.partial(kernel, halves, inner, feats, turn), in_...  44.5 us

profile of v3, /device:TPU:0, one launch (start us, length us, event | category | flops | bytes accessed | tf_op | source)
XLA Modules:
  0.0 45.2 jit_solution(434733486038946610)
XLA Ops:
  0.0 44.5 %shard_map.46 = f32[4,64,256]{2,1,0:T(8,128)S(1)} custom-call(s32[512,1024]{1,0:T(8,128)} %given_ref.1, f32[1,1024]{1,0:T(1,128)} %bitcast.3, s32[1,512]{1,0:T(1,128)} %bitcast.4, s32[1,512]{1,0:T(1,128)} %bitcast.5), custom_call_target="tpu_custom_call" | custom-call | tf_op jit(solution)/shard_map/pallas_call | solution.py:416
  44.5 0.7 %copy.6 = f32[4,64,256]{2,1,0:T(8,128)} copy(f32[4,64,256]{2,1,0:T(8,128)S(1)} %shard_map.46) | data formatting | bytes 524288

commit v4 on v3

--- a/solution.py
+++ b/solution.py
@@ -278,7 +278,6 @@
         def _():
             send_chunk(chunk + AHEAD)
 
-        acc_ref[...] = jnp.zeros_like(acc_ref)
         own_copy(chunk).wait()
 
         def batch_step(j):
@@ -334,7 +333,7 @@
                             0,
                         )
                     )
-                acc_ref[f] += lax.dot_general(
+                acc_ref[f] = jnp.where(j == 0, 0.0, acc_ref[f]) + lax.dot_general(
                     jnp.concatenate(aa, 1),
                     jnp.concatenate(bb, 1),
                     (((1,), (1,)), ((), ())),

time: 45.3 us -> 45.3 us (level)
  no operation moved by 1% of the time
where the time goes in v4:
time: 45.3 us; the launch traced here: 45.2 us
  Pallas kernels  44.5 us (98%)
  local copies, waits for them, and re-layouts  0.71 us (2%)
    pallas_call x1, Pallas kernels, shards(): pl.pallas_call(functools.partial(kernel, halves, inner, feats, turn), in_...  44.5 us

profile of v4, /device:TPU:0, one launch (start us, length us, event | category | flops | bytes accessed | tf_op | source)
XLA Modules:
  0.0 45.2 jit_solution(15706888133865241377)
XLA Ops:
  0.0 44.5 %shard_map.46 = f32[4,64,256]{2,1,0:T(8,128)S(1)} custom-call(s32[512,1024]{1,0:T(8,128)} %given_ref.1, f32[1,1024]{1,0:T(1,128)} %bitcast.3, s32[1,512]{1,0:T(1,128)} %bitcast.4, s32[1,512]{1,0:T(1,128)} %bitcast.5), custom_call_target="tpu_custom_call" | custom-call | tf_op jit(solution)/shard_map/pallas_call | solution.py:415
  44.5 0.7 %copy.6 = f32[4,64,256]{2,1,0:T(8,128)} copy(f32[4,64,256]{2,1,0:T(8,128)S(1)} %shard_map.46) | data formatting | bytes 524288
